TPU v7x, 512 devices: a whole 4x4x16 slice. The times are simulated.
512 devices in a mesh: lat: 64 (over z, y), wid: 2 (over core), tok: 4 (over x).
Axes of the slice: x: 4, y: 4, z: 16, core: 2. Of those that a mesh axis runs over, the one named last changes fastest.
Arguments:
- resid: bfloat16 [512, 4096], P('tok', 'wid'), may hold values from -6 to 6
- dictionary: bfloat16 [32768, 4096], P('lat', 'wid'), may hold values from -0.1875 to 0.1875
- enc_bias: float32 [32768], P('lat'), may hold values from -3 to 3
- dec_bias: float32 [4096], P('wid'), may hold values from -3 to 3
- active_blocks: int32 [512, 8], P('tok'), may hold values from 0 to 255, all different within a row
- level_bounds: int32 [4], replicated, may hold values from 1 to 256, as said below
Outputs:
- level_losses: float32 [4], replicated
- dict_grad: bfloat16 [4096, 32768], P(('wid', 'tok'), 'lat')
Inputs may be any that keep to these rules, and one draw needn't show every extreme that they name: `active_blocks`: each row names 8 different blocks. `level_bounds`: strictly increasing; the last equals 256.
All inputs are finite; a program needn't handle non-finite values.
Results may differ from a plain program's by a relative error of at most 0.006.
Values sent between devices are 32-bit elements; how exact they have to be, the bound alone decides.
A program may use at most 192 MiB of HBM per device.

v0:
```python
import jax
import jax.numpy as jnp
from jax import lax
from jax.sharding import PartitionSpec as P

LEVELS = 4


def entering(part, axis, combine, identity):
    place = lax.axis_index(axis)
    gathered = lax.all_gather(part, axis)
    state = jnp.zeros_like(part) + jnp.asarray(identity, part.dtype)

    def one(turn, state):
        return combine(state, lax.dynamic_index_in_dim(gathered, turn, 0, False))

    return lax.fori_loop(0, place, one, state)


def broadcast(array, axis, root):
    mine = lax.axis_index(axis) == root
    return lax.psum(jnp.where(mine, array, jnp.zeros_like(array)), axis)


def gelu_tanh(value):
    return jax.nn.gelu(value, approximate=True)


def add_pair(earlier, later):
    return earlier + later


def body(resid, dictionary, enc_bias, dec_bias, active_blocks, level_bounds):
    row_count, half_width = resid.shape
    lat_count = dictionary.shape[0]
    blocks_here = lat_count // 128
    lat_position = lax.axis_index("lat")
    first_block = lat_position * blocks_here
    local_ids = first_block + jnp.arange(blocks_here, dtype=jnp.int32)
    resid_full = resid.astype(jnp.float32)
    dict_blocks = dictionary.reshape(blocks_here, 128, half_width)
    partial_pre = lax.dot_general(
        resid, dictionary, (((1,), (1,)), ((), ())), preferred_element_type=jnp.float32
    )
    pre = lax.psum(partial_pre, "wid") + enc_bias[None, :]
    hits = jnp.any(active_blocks[:, :, None] == local_ids[None, None, :], axis=1).astype(
        jnp.float32
    )
    act = (gelu_tanh(pre).reshape(row_count, blocks_here, 128) * hits[:, :, None]).astype(
        jnp.bfloat16
    )
    act_flat = act.reshape(row_count, lat_count)
    latent_block = jnp.arange(lat_count, dtype=jnp.int32) // 128
    owners = []
    keeps = []
    for level in range(LEVELS):
        bound = level_bounds[level]
        owners.append((bound - 1) // blocks_here)
        inside = jnp.clip(bound - 1 - first_block, 0, blocks_here - 1)
        keeps.append(latent_block <= inside)
    keeps.append(latent_block >= 0)
    keep_rows = jnp.stack(keeps)
    act_stack = jnp.where(keep_rows[:, None, :], act_flat[None], jnp.zeros((), jnp.bfloat16))
    partials = jnp.dot(
        act_stack.reshape((LEVELS + 1) * row_count, lat_count),
        dictionary,
        preferred_element_type=jnp.float32,
    )
    partials = partials.reshape(LEVELS + 1, row_count, half_width)
    zeros_field = jnp.zeros((row_count, half_width), jnp.float32)
    earlier = entering(partials[LEVELS], "lat", add_pair, zeros_field)
    own_errors = []
    squares = []
    for level in range(LEVELS):
        mine = owners[level] == lat_position
        error = dec_bias[None, :] + earlier + partials[level] - resid_full
        own_errors.append(jnp.where(mine, error, 0.0))
        squares.append(jnp.where(mine, jnp.sum(error * error), 0.0))
    include = (level_bounds[:, None] > local_ids[None, :]).astype(jnp.float32)
    err_sum = None
    for level in range(LEVELS):
        level_err = broadcast(own_errors[level], "lat", owners[level])
        term = include[level][:, None, None] * level_err[None]
        err_sum = term if err_sum is None else err_sum + term
    err_half = err_sum.astype(jnp.bfloat16)
    partial_adjoint = jnp.einsum(
        "ktd,kcd->tkc", err_half, dict_blocks, preferred_element_type=jnp.float32
    )
    g_act = lax.psum(partial_adjoint.reshape(row_count, lat_count), "wid")
    mask_full = jnp.broadcast_to(hits[:, :, None], (row_count, blocks_here, 128)).reshape(
        row_count, lat_count
    )
    _, pull = jax.vjp(gelu_tanh, pre)
    g_pre = pull(g_act * mask_full)[0].astype(jnp.bfloat16)
    decode_term = jnp.einsum("ktd,tkc->dkc", err_half, act, preferred_element_type=jnp.float32)
    encode_term = lax.dot_general(
        resid, g_pre, (((0,), (0,)), ((), ())), preferred_element_type=jnp.float32
    )
    grad_share = lax.psum_scatter(
        decode_term.reshape(half_width // lax.axis_size("tok") * lax.axis_size("tok"), lat_count)
        + encode_term,
        "tok",
        scatter_dimension=0,
        tiled=True,
    )
    total_sq = lax.psum(jnp.stack(squares), ("lat", "wid", "tok"))
    level_losses = total_sq / (row_count * lax.axis_size("tok") * half_width * lax.axis_size("wid"))
    return (level_losses, grad_share.astype(jnp.bfloat16))


def solution(mesh):
    return jax.shard_map(
        body,
        mesh=mesh,
        in_specs=(P("tok", "wid"), P("lat", "wid"), P("lat"), P("wid"), P("tok", None), P()),
        out_specs=(P(), P(("wid", "tok"), "lat")),
        check_vma=False,
    )
```

profile of v0, /device:TPU:1, one launch (start us, length us, event | category | flops | bytes accessed | tf_op | source)
XLA Modules:
  0.0 1121.9 jit_solution(13684418029557174763)
XLA Ops:
  7.2 1.5 copy-done
  8.8 2.6 fusion.25
  11.4 1.5 fusion.23
  12.9 0.8 compare_reduce_fusion
  16.4 41.2 %all-reduce.5.cloned.1.call-done = f32[128,512]{1,0:T(8,128)} async-done(((f32[128,512]{1,0:T(8,128)}), f32[128,512]{1,0:T(8,128)}) %all-reduce.5.cloned.1.call-update) | async-done | bytes 262160 | tf_op jit(solution)/shard_map/psum | solution.py:45
  57.6 1.8 multiply_convert_fusion.1
  59.4 1.6 fusion.26
  61.0 2.3 copy-done.1
  63.3 1.1 slice.60
  64.6 512.8 %all-gather.3.cloned.1.call-done = f32[8192,2048]{1,0:T(8,128)} async-done(((f32[128,2048]{1,0:T(8,128)}), f32[8192,2048]{1,0:T(8,128)}) %all-gather.3.cloned.1.call-update) | async-done | bytes 67108880 | tf_op jit(solution)/shard_map/all_gather | solution.py:11
  577.6 0.7 copy-done.6
  578.2 5.8 select_select_fusion.3
  584.1 0.6 copy-done.5
  584.7 0.2 copy-done.3
  585.1 365.0 %all-reduce.9.cloned.1.call-done = (f32[128,2048]{1,0:T(8,128)}, f32[128,2048]{1,0:T(8,128)}, f32[128,2048]{1,0:T(8,128)}, f32[128,2048]{1,0:T(8,128)}) async-done(((f32[128,2048]{1,0:T(8,128)}, f32[128,2048]{1,0:T(8,128)}, f32[128,2048]{1,0:T(8,128)}, f32[128,2048]{1,0:T(8,128)}), (f32[128,2048]{1,0:T(8,128)}, f32[128,2048]{1,0:T(8,128)}, f32[128,2048]{1,0:T(8,128)}, ...) | async-done | bytes 4194320 | tf_op jit(solution)/shard_map/psum | solution.py:22
  950.1 3.5 fusion.24
  953.6 0.8 copy.19
  954.6 5.7 fusion.7
  960.2 39.1 %all-reduce.7.cloned.1.call-done = f32[128,512]{1,0:T(8,128)} async-done(((f32[128,512]{1,0:T(8,128)}), f32[128,512]{1,0:T(8,128)}) %all-reduce.7.cloned.1.call-update) | async-done | bytes 262160 | tf_op jit(solution)/shard_map/psum | solution.py:89
  999.3 5.1 bitcast_add_fusion.1
  1007.1 105.4 %psum.50 = f32[4]{0:T(128)S(1)} all-reduce(f32[4]{0:T(128)S(1)} %pad_maximum_fusion), channel_id=1, replica_groups=mesh['lat'=64,'wid'=2,'tok'=4] {'lat','wid','tok'}, use_global_device_ids=true, to_apply=%region_8.9 | all-reduce | flops 4 | bytes 32 | tf_op jit(solution)/shard_map/psum | solution.py:106
  1112.6 0.5 broadcast_multiply_fusion
  1113.1 1.3 convert_element_type.36
  1114.4 1.0 copy.16
  (37 shorter events, 1.0 us)
Async XLA Ops:
  7.2 1.6 copy-start
  7.2 50.4 %all-reduce.5.cloned.1.call-start = ((), (), s32[]{:S(2)}) async-start(), calls=%async_computation.1 | async-start | bytes 524288 | tf_op jit(solution)/shard_map/psum | solution.py:45
  11.4 566.1 %all-gather.3.cloned.1.call-start = ((), (), s32[]{:S(2)}) async-start(), calls=%async_computation.4 | async-start | bytes 68157440 | tf_op jit(solution)/shard_map/all_gather | solution.py:11
  61.0 2.3 copy-start.1
  64.4 885.7 %all-reduce.9.cloned.1.call-start = ((), (), s32[]{:S(2)}) async-start(), calls=%async_computation.5 | async-start | bytes 8388608 | tf_op jit(solution)/shard_map/psum | solution.py:22
  577.5 0.7 copy-start.6
  584.0 0.7 copy-start.5
  584.0 1.0 copy-start.3
  584.0 415.3 %all-reduce.7.cloned.1.call-start = ((), (), s32[]{:S(2)}) async-start(), calls=%async_computation.2 | async-start | bytes 524288 | tf_op jit(solution)/shard_map/psum | solution.py:89
  954.5 158.6 %reduce-scatter.2.cloned.1.call-start = ((), (), s32[]{:S(2)}) async-start(), calls=%async_computation.3 | async-start | bytes 5242880 | tf_op jit(solution)/shard_map/reduce_scatter | solution.py:99
  954.5 44.8 %copy-start.2 = (bf16[128,2048]{1,0:T(8,128)(2,1)S(1)}, bf16[128,2048]{1,0:T(8,128)(2,1)}, u32[]{:S(2)}) copy-start(bf16[128,2048]{1,0:T(8,128)(2,1)} %param.8) | copy-start | bytes 1572868
  954.5 44.8 %copy-start.4 = (f32[128,512]{1,0:T(8,128)S(1)}, f32[128,512]{1,0:T(8,128)}, u32[]{:S(2)}) copy-start(f32[128,512]{1,0:T(8,128)} %all-reduce.5.cloned.1.call-done) | copy-start | bytes 786436
  954.5 44.8 %copy-start.7 = (f32[512]{0:T(512)S(1)}, f32[512]{0:T(512)}, u32[]{:S(2)}) copy-start(f32[512]{0:T(512)} %param.10) | copy-start | bytes 6148
Sparse Core Ops, SparseCore 0:
  11.5 46.0 all-reduce.4
  64.6 512.8 all-gather.2
  584.2 365.8 all-reduce.8
  954.6 44.6 all-reduce.6
  1004.6 54.7 reduce-scatter.1
where the time goes:
time: 1120 us
  waiting for transfers between devices  958 us (86%)
  blocking collectives  105 us (9%)
  between operations  19.2 us (2%)
  matrix products  18.4 us (2%)
    all_gather x1, waiting for transfers between devices, entering(): gathered = lax.all_gather(part, axis)  513 us
    psum x1, waiting for transfers between devices, broadcast(): return lax.psum(jnp.where(mine, array, jnp.zeros_like(array)), axis)  365 us
    psum x1, blocking collectives, body(): total_sq = lax.psum(jnp.stack(squares), ('lat', 'wid', 'tok'))  105 us
    psum x1, waiting for transfers between devices, body(): pre = lax.psum(partial_pre, 'wid') + enc_bias[None, :]  41.2 us
    psum x1, waiting for transfers between devices, body(): g_act = lax.psum(partial_adjoint.reshape(row_count, lat_count), 'wid')  39.1 us
  transfers between devices with their start and end apart: 5, of which 4 were waited for; matrix products, arithmetic and copies ran while one was open for 1% of the time, Pallas kernels for 0%

commit v1 on v0

--- a/solution.py
+++ b/solution.py
@@ -103,7 +103,9 @@
         scatter_dimension=0,
         tiled=True,
     )
-    total_sq = lax.psum(jnp.stack(squares), ("lat", "wid", "tok"))
+    chunk = jnp.stack(squares)
+    last = lax.all_gather(chunk, axis_name=("lat", "wid", "tok"))
+    total_sq = jnp.sum(last, axis=0)
     level_losses = total_sq / (row_count * lax.axis_size("tok") * half_width * lax.axis_size("wid"))
     return (level_losses, grad_share.astype(jnp.bfloat16))
 

time: 1120 us -> 1130 us (level)
    unnamed x0 -> x1, blocking collectives: none -> 105 us
    psum x1 -> x0, blocking collectives: 105 us -> none  [body(): total_sq = lax.psum(jnp.stack(squares), ('lat', 'wid', 'tok'))]
where the time goes in v1:
time: 1130 us; the launch traced here: 1120 us
  waiting for transfers between devices  958 us (85%)
  blocking collectives  105 us (9%)
  between operations  19 us (2%)
  matrix products  18.4 us (2%)
    all_gather x1, waiting for transfers between devices, entering(): gathered = lax.all_gather(part, axis)  513 us
    psum x1, waiting for transfers between devices, broadcast(): return lax.psum(jnp.where(mine, array, jnp.zeros_like(array)), axis)  365 us
    unnamed x1, blocking collectives  105 us
    psum x1, waiting for transfers between devices, body(): pre = lax.psum(partial_pre, 'wid') + enc_bias[None, :]  41.1 us
    psum x1, waiting for transfers between devices, body(): g_act = lax.psum(partial_adjoint.reshape(row_count, lat_count), 'wid')  39.1 us
  transfers between devices with their start and end apart: 5, of which 4 were waited for; matrix products, arithmetic and copies ran while one was open for 1% of the time, Pallas kernels for 0%

profile of v1, /device:TPU:1, one launch (start us, length us, event | category | flops | bytes accessed | tf_op | source)
XLA Modules:
  0.0 1122.6 jit_solution(13241242316353111017)
XLA Ops:
  7.2 1.5 copy-done
  8.8 2.6 fusion.25
  11.4 1.5 fusion.23
  12.9 0.8 compare_reduce_fusion
  16.5 41.1 %all-reduce.6.cloned.1.call-done = f32[128,512]{1,0:T(8,128)} async-done(((f32[128,512]{1,0:T(8,128)}), f32[128,512]{1,0:T(8,128)}) %all-reduce.6.cloned.1.call-update) | async-done | bytes 262160 | tf_op jit(solution)/shard_map/psum | solution.py:45
  57.6 1.8 multiply_convert_fusion.1
  59.4 1.6 fusion.26
  61.0 2.3 copy-done.1
  63.3 1.1 slice.60
  64.6 512.8 %all-gather.4.cloned.1.call-done = f32[8192,2048]{1,0:T(8,128)} async-done(((f32[128,2048]{1,0:T(8,128)}), f32[8192,2048]{1,0:T(8,128)}) %all-gather.4.cloned.1.call-update) | async-done | bytes 67108880 | tf_op jit(solution)/shard_map/all_gather | solution.py:11
  577.6 0.7 copy-done.6
  578.3 5.7 select_select_fusion.3
  584.1 0.6 copy-done.5
  585.1 365.3 %all-reduce.10.cloned.1.call-done = (f32[128,2048]{1,0:T(8,128)}, f32[128,2048]{1,0:T(8,128)}, f32[128,2048]{1,0:T(8,128)}, f32[128,2048]{1,0:T(8,128)}) async-done(((f32[128,2048]{1,0:T(8,128)}, f32[128,2048]{1,0:T(8,128)}, f32[128,2048]{1,0:T(8,128)}, f32[128,2048]{1,0:T(8,128)}), (f32[128,2048]{1,0:T(8,128)}, f32[128,2048]{1,0:T(8,128)}, f32[128,2048]{1,0:T(8,128)}, ...) | async-done | bytes 4194320 | tf_op jit(solution)/shard_map/psum | solution.py:22
  950.4 3.5 fusion.24
  953.9 0.8 copy.24
  954.9 5.7 fusion.7
  960.5 39.1 %all-reduce.8.cloned.1.call-done = f32[128,512]{1,0:T(8,128)} async-done(((f32[128,512]{1,0:T(8,128)}), f32[128,512]{1,0:T(8,128)}) %all-reduce.8.cloned.1.call-update) | async-done | bytes 262160 | tf_op jit(solution)/shard_map/psum | solution.py:89
  999.6 5.1 bitcast_add_fusion.1
  1007.4 105.5 %all-reduce = f32[2048]{0:T(1024)S(1)} all-reduce(f32[2048]{0:T(1024)S(1)} %maximum_dynamic-update-slice_fusion), channel_id=3, replica_groups=mesh['lat'=64,'wid'=2,'tok'=4] {'lat','wid','tok'}, use_global_device_ids=true, to_apply=%add | all-reduce | flops 2048 | bytes 16384
  1112.9 0.3 reshape.130
  1113.2 0.5 broadcast_multiply_fusion
  1113.7 1.3 convert_element_type.36
  1115.0 1.0 copy.21
  (40 shorter events, 1.4 us)
Async XLA Ops:
  7.2 1.6 copy-start
  7.2 50.4 %all-reduce.6.cloned.1.call-start = ((), (), s32[]{:S(2)}) async-start(), calls=%async_computation.1 | async-start | bytes 524288 | tf_op jit(solution)/shard_map/psum | solution.py:45
  11.4 566.1 %all-gather.4.cloned.1.call-start = ((), (), s32[]{:S(2)}) async-start(), calls=%async_computation.4 | async-start | bytes 68157440 | tf_op jit(solution)/shard_map/all_gather | solution.py:11
  61.0 2.3 copy-start.1
  64.5 885.9 %all-reduce.10.cloned.1.call-start = ((), (), s32[]{:S(2)}) async-start(), calls=%async_computation.5 | async-start | bytes 8388608 | tf_op jit(solution)/shard_map/psum | solution.py:22
  577.6 0.7 copy-start.6
  584.0 0.7 copy-start.5
  584.0 1.0 copy-start.3
  584.0 415.6 %all-reduce.8.cloned.1.call-start = ((), (), s32[]{:S(2)}) async-start(), calls=%async_computation.2 | async-start | bytes 524288 | tf_op jit(solution)/shard_map/psum | solution.py:89
  954.8 159.0 %reduce-scatter.2.cloned.1.call-start = ((), (), s32[]{:S(2)}) async-start(), calls=%async_computation.3 | async-start | bytes 5242880 | tf_op jit(solution)/shard_map/reduce_scatter | solution.py:99
  954.8 44.8 %copy-start.2 = (bf16[128,2048]{1,0:T(8,128)(2,1)S(1)}, bf16[128,2048]{1,0:T(8,128)(2,1)}, u32[]{:S(2)}) copy-start(bf16[128,2048]{1,0:T(8,128)(2,1)} %param.8) | copy-start | bytes 1572868
  954.8 44.8 %copy-start.4 = (f32[128,512]{1,0:T(8,128)S(1)}, f32[128,512]{1,0:T(8,128)}, u32[]{:S(2)}) copy-start(f32[128,512]{1,0:T(8,128)} %all-reduce.6.cloned.1.call-done) | copy-start | bytes 786436
  954.8 44.8 %copy-start.7 = (f32[512]{0:T(512)S(1)}, f32[512]{0:T(512)}, u32[]{:S(2)}) copy-start(f32[512]{0:T(512)} %param.10) | copy-start | bytes 6148
Sparse Core Ops, SparseCore 0:
  11.5 46.0 all-reduce.5
  64.6 512.8 all-gather.3
  584.1 366.2 all-reduce.9
  954.9 44.6 all-reduce.7
  1004.9 54.7 reduce-scatter.1
